TPU v7x, 256 devices: a whole 4x4x8 slice. The times are simulated.
256 devices in a mesh: kv: 2 (over y_hi), blk: 128 (over x, y_lo, z, core).
Axes of the slice: x: 4, y: 4 (y_hi: 2, y_lo: 2; y = y_hi * 2 + y_lo), z: 8, core: 2. Of those that a mesh axis runs over, the one named last changes fastest.
Arguments:
- hidden_in: bfloat16 [65536, 1280], P('blk'), may hold values from -6 to 6
- w_query: bfloat16 [1280, 1280], P(None, 'kv'), may hold values from -0.15625 to 0.15625
- w_key: bfloat16 [1280, 1280], P(None, 'kv'), may hold values from -0.15625 to 0.15625
- w_value: bfloat16 [1280, 1280], P(None, 'kv'), may hold values from -0.15625 to 0.15625
- w_out: bfloat16 [1280, 1280], P('kv'), may hold values from -0.15625 to 0.15625
- head_gain: float32 [1280], P('kv'), may hold values from 1 to 2.5
- eigen_rate: float32 [1280], replicated, may hold values from 0.15 to 0.6
- pool_keys: bfloat16 [512, 256, 1280], P('blk', None, 'kv'), may hold values from -2 to 2
- pool_values: bfloat16 [512, 256, 1280], P('blk', None, 'kv'), may hold values from -6 to 6
- req_len: int32 [128], P('blk'), may hold values from 1 to 512, as said below
- prefix_len: int32 [128], P('blk'), may hold values from 0 to 4, as said below
- prefix_pages: int32 [128, 4], replicated, may hold values from 0 to 511, as said below
- placement: int32 [256], replicated, may hold values from 0 to 255, as said below
Outputs:
- layer_out: bfloat16 [65536, 1280], P('blk')
- new_keys: bfloat16 [256, 256, 1280], P('blk', None, 'kv')
- new_values: bfloat16 [256, 256, 1280], P('blk', None, 'kv')
Inputs may be any that keep to these rules, and one draw needn't show every extreme that they name: `req_len`: some request has all 512 tokens live. `prefix_len`: some request has 4 cached pages. Page prefix_pages[r, s] lies among pages h * 4 to (h + 1) * 4 - 1 with h = (r + 1 + s * 32) mod 128, for every slot s. Each page once; placement[b] lies among pages e * 2 to (e + 1) * 2 - 1 with e = (b // 2 + (2 * (b mod 2) + 1) * 32) mod 128.
All inputs are finite; a program needn't handle non-finite values.
Results may differ from a plain program's by a relative error of at most 0.0067.
Values may be sent and summed in bfloat16 or wider, within the bound.
A program may use at most 128 MiB of HBM per device.

v0:
```python
import math
import jax
import jax.numpy as jnp
from jax import lax
from jax.sharding import PartitionSpec as P

HD = 64
PAGE = 256
PMAX = 4
epsilon = 1e-06


def from_behind(block, axis, distance):
    devices = range(lax.axis_size(axis))
    route = [((i - distance) % len(devices), i) for i in devices]
    return lax.ppermute(block, axis, route)


def rms_scale(values):
    return values * lax.rsqrt(jnp.mean(values * values, axis=-1, keepdims=True) + epsilon)


def head_normed(projected, head_gain):
    count = projected.shape[0]
    split_heads = projected.reshape(count, -1, HD)
    return (rms_scale(split_heads).reshape(count, -1) * head_gain).astype(jnp.bfloat16)


def attend(query_heads, key_rows, value_rows, visible):
    key_heads = key_rows.reshape(key_rows.shape[0], -1, HD)
    value_heads = value_rows.reshape(value_rows.shape[0], -1, HD)
    scores = jnp.einsum(
        "qhd,khd->hqk", query_heads, key_heads, preferred_element_type=jnp.float32
    ) / math.sqrt(HD)
    weights = jnp.where(visible, jnp.exp(scores), 0.0)
    totals = jnp.sum(weights, axis=-1)
    mixed = jnp.einsum(
        "hqk,khd->qhd",
        weights.astype(jnp.bfloat16),
        value_heads,
        preferred_element_type=jnp.float32,
    )
    return (totals, mixed)


def fetch_page(pool_keys, pool_values, prefix_pages, slot_index):
    devices = lax.axis_size("blk")
    here = lax.axis_index("blk")
    offset = slot_index * devices // PMAX + 1
    asker = (here - offset) % devices
    local = prefix_pages[asker, slot_index] % pool_keys.shape[0]
    send_keys = lax.dynamic_index_in_dim(pool_keys, local, 0, keepdims=False)
    send_values = lax.dynamic_index_in_dim(pool_values, local, 0, keepdims=False)
    return from_behind((send_keys, send_values), "blk", devices - offset)


def relay(key_rows, value_rows, placement):
    devices = lax.axis_size("blk")
    here = lax.axis_index("blk")
    blocks = key_rows.shape[0] // PAGE
    width = key_rows.shape[1]
    key_pages = key_rows.reshape(blocks, PAGE, width)
    value_pages = value_rows.reshape(blocks, PAGE, width)
    key_out = jnp.zeros_like(key_pages)
    value_out = jnp.zeros_like(value_pages)
    for block_index in range(blocks):
        offset = (2 * block_index + 1) * devices // (2 * blocks)
        key_recv, value_recv = from_behind(
            (key_pages[block_index], value_pages[block_index]), "blk", offset
        )
        source = (here - offset) % devices
        target = placement[source * blocks + block_index] % blocks
        key_out = lax.dynamic_update_index_in_dim(key_out, key_recv, target, 0)
        value_out = lax.dynamic_update_index_in_dim(value_out, value_recv, target, 0)
    return (key_out, value_out)


def body(
    hidden_in,
    w_query,
    w_key,
    w_value,
    w_out,
    head_gain,
    eigen_rate,
    pool_keys,
    pool_values,
    req_len,
    prefix_len,
    prefix_pages,
    placement,
):
    tokens_here = hidden_in.shape[0]
    width_half = w_query.shape[1]
    heads_here = width_half // HD
    hidden_f = hidden_in.astype(jnp.float32)
    row_scale = lax.rsqrt(jnp.mean(hidden_f * hidden_f, axis=-1, keepdims=True) + epsilon)
    anchor = hidden_f * row_scale
    queries = head_normed(
        jnp.dot(hidden_in, w_query, preferred_element_type=jnp.float32), head_gain
    )
    key_rows = head_normed(jnp.dot(hidden_in, w_key, preferred_element_type=jnp.float32), head_gain)
    value_rows = (
        jnp.dot(hidden_in, w_value, preferred_element_type=jnp.float32) * row_scale
    ).astype(jnp.bfloat16)
    live_count = req_len[0]
    depth = prefix_len[0]
    query_heads = queries.reshape(tokens_here, heads_here, HD)
    row_index = jnp.arange(tokens_here, dtype=jnp.int32)[:, None]
    col_index = jnp.arange(tokens_here, dtype=jnp.int32)[None, :]
    own_visible = ((col_index <= row_index) & (col_index < live_count))[None]
    totals, mixed = attend(query_heads, key_rows, value_rows, own_visible)
    fetched_keys = []
    fetched_values = []
    for slot_index in range(PMAX):
        page_keys, page_values = fetch_page(pool_keys, pool_values, prefix_pages, slot_index)
        fetched_keys.append(page_keys)
        fetched_values.append(page_values)
    cached_keys = jnp.concatenate(fetched_keys, axis=0)
    cached_values = jnp.concatenate(fetched_values, axis=0)
    page_number = jnp.arange(cached_keys.shape[0], dtype=jnp.int32) // PAGE
    cached_visible = (page_number < depth)[None, None, :]
    more_totals, more_mixed = attend(query_heads, cached_keys, cached_values, cached_visible)
    totals = totals + more_totals
    mixed = mixed + more_mixed
    attended = (mixed / totals.T[:, :, None]).astype(jnp.bfloat16).reshape(tokens_here, width_half)
    partial_branch = jnp.dot(attended, w_out, preferred_element_type=jnp.float32)
    branch = lax.psum(partial_branch, "kv")
    updated = anchor + eigen_rate * (rms_scale(branch) - anchor)
    layer_out = rms_scale(updated).astype(jnp.bfloat16)
    new_keys, new_values = relay(key_rows, value_rows, placement)
    return (layer_out, new_keys, new_values)


def solution(mesh):
    in_specs = (
        P("blk", None),
        P(None, "kv"),
        P(None, "kv"),
        P(None, "kv"),
        P("kv", None),
        P("kv"),
        P(),
        P("blk", None, "kv"),
        P("blk", None, "kv"),
        P("blk"),
        P("blk"),
        P(),
        P(),
    )
    out_specs = (P("blk", None), P("blk", None, "kv"), P("blk", None, "kv"))
    return jax.shard_map(body, mesh=mesh, in_specs=in_specs, out_specs=out_specs, check_vma=False)
```

profile of v0, /device:TPU:1, one launch (start us, length us, event | category | flops | bytes accessed | tf_op | source)
XLA Modules:
  0.0 205.1 jit_solution(14092505884325169063)
XLA Ops:
  7.2 0.0 copy-start
  7.2 0.0 all-reduce.2.cloned.1.call-start
  7.3 1.4 constant_dynamic-slice_fusion
  16.5 0.0 copy-start.8
  16.5 2.5 %dynamic-slice_bitcast_fusion.3 = (bf16[256,640]{1,0:T(8,128)(2,1)}, bf16[256,640]{1,0:T(8,128)(2,1)}, bf16[256,640]{1,0:T(8,128)(2,1)}, bf16[256,640]{1,0:T(8,128)(2,1)}) fusion(bf16[4,256,640]{2,1,0:T(8,128)(2,1)} %param.20, s32[]{:T(128)S(6)} %select_n.116, s32[]{:T(128)S(6)} %select_n.120, s32[]{:T(128)S(6)} %select_n.128, s32[]{:T(128)S(6)} %select_n.124), kind=kLoop, calls=%fused_computation.39 | loop fusion | bytes 2621456 | tf_op jit(solution)/shard_map/jit(dynamic_index_in_dim)/squeeze | solution.py:52
  19.0 3.2 %collective-permute-start.4 = (bf16[256,640]{1,0:T(8,128)(2,1)}, bf16[256,640]{1,0:T(8,128)(2,1)S(1)}, u32[]{:S(2)}, u32[]{:S(2)}) collective-permute-start(bf16[256,640]{1,0:T(8,128)(2,1)} %get-tuple-element.3), channel_id=1, source_target_pairs={{1,0},{2,1},{3,2},{4,3},{5,4},{6,5},{7,6},{8,7},{9,8},{10,9},{11,1... | collective-permute-start | bytes 983048 | tf_op jit(solution)/shard_map/ppermute | solution.py:16
  22.3 7.2 %collective-permute-start.5 = (bf16[256,640]{1,0:T(8,128)(2,1)}, bf16[256,640]{1,0:T(8,128)(2,1)}, u32[]{:S(2)}, u32[]{:S(2)}) collective-permute-start(bf16[256,640]{1,0:T(8,128)(2,1)} %get-tuple-element.4), channel_id=1, source_target_pairs={{33,0},{34,1},{35,2},{36,3},{37,4},{38,5},{39,6},{40,7},{41,8},{42... | collective-permute-start | bytes 983048 | tf_op jit(solution)/shard_map/ppermute | solution.py:16
  29.5 0.9 collective-permute-start.7
  30.4 0.3 collective-permute-start.6
  30.7 1.1 dynamic-slice_bitcast_fusion.7
  32.5 0.3 fusion.15
  32.9 0.1 fusion.23
  33.0 2.0 fusion.22
  35.0 2.2 %copy.21 = bf16[512,640]{0,1:T(8,128)(2,1)} copy(bf16[512,640]{1,0:T(8,128)(2,1)} %fusion.22) | data formatting | bytes 1310720 | tf_op jit(solution)/shard_map/convert_element_type | solution.py:105
  37.2 2.7 %fusion.38 = (f32[512,640]{1,0:T(8,128)}, f32[512,640]{1,0:T(8,128)}) fusion(bf16[512,1280]{1,0:T(8,128)(2,1)S(1)} %copy-done.3, bf16[1280,640]{1,0:T(8,128)(2,1)S(1)} %copy-done), kind=kOutput, calls=%fused_computation.71 | convolution fusion | flops 839188480 | bytes 5570560 | tf_op jit(solution)/shard_map/dot_general | solution.py:100
  39.9 1.7 copy.22
  41.6 0.2 reduce_sum.64
  41.8 0.1 mul.111
  41.9 1.5 copy.23
  43.4 4.1 %fusion.37 = (f32[512,640]{1,0:T(8,128)}, f32[512,640]{1,0:T(8,128)}) fusion(bf16[512,1280]{1,0:T(8,128)(2,1)S(1)} %copy-done.3, bf16[1280,640]{1,0:T(8,128)(2,1)} %param.15), kind=kOutput, calls=%fused_computation.70 | convolution fusion | flops 839188480 | bytes 5570560 | tf_op jit(solution)/shard_map/dot_general | solution.py:102
  47.5 1.7 copy.25
  49.2 0.2 reduce_sum.65
  49.4 0.1 mul.118
  49.6 0.0 copy-start.15
  49.6 1.5 copy.26
  51.0 2.8 %multiply_convert_fusion.1 = (bf16[512,640]{1,0:T(8,128)(2,1)S(1)}, bf16[512,640]{1,0:T(8,128)(2,1)S(1)}) fusion(f32[512,640]{1,0:T(8,128)} %get-tuple-element.24, f32[512,640]{1,0:T(8,128)} %copy.26, f32[640]{0:T(1024)S(1)} %copy-done.15, f32[512,640]{1,0:T(8,128)} %get-tuple-element.26, f32[512,640]{1,0:T(8,128)} %copy.23), kind=kLoop, calls=%fused_computation.28 | loop fusion | flops 1966080 | bytes 6556160 | tf_op jit(solution)/shard_map/convert_element_type | solution.py:26
  53.8 1.1 copy.24
  54.9 1.1 copy.27
  56.0 4.7 %fusion.5 = (f32[10,512]{1,0:T(8,128)}, f32[10,512,512]{1,2,0:T(8,128)S(1)}) fusion(pred[512,512]{0,1:T(8,128)(4,1)S(1)} %fusion.23, bf16[512,10,64]{0,2,1:T(8,128)(2,1)} %bitcast.71, bf16[512,10,64]{0,2,1:T(8,128)(2,1)} %bitcast.73), kind=kOutput, calls=%fused_computation.6 | convolution fusion | flops 343403520 | bytes 12079104 | tf_op jit(solution)/shard_map/qhd,khd->hqk/dot_general | solution.py:32
  60.7 2.8 %collective-permute-start.1 = (bf16[256,640]{1,0:T(8,128)(2,1)}, bf16[256,640]{1,0:T(8,128)(2,1)}, u32[]{:S(2)}, u32[]{:S(2)}) collective-permute-start(bf16[256,640]{1,0:T(8,128)(2,1)} %get-tuple-element.8), channel_id=1, source_target_pairs={{33,0},{34,1},{35,2},{36,3},{37,4},{38,5},{39,6},{40,7},{41,8},{42... | collective-permute-start | bytes 983048 | tf_op jit(solution)/shard_map/ppermute | solution.py:16
  63.6 0.8 collective-permute-start.3
  64.4 2.7 %collective-permute-start.2 = (bf16[256,640]{1,0:T(8,128)(2,1)S(1)}, bf16[256,640]{1,0:T(8,128)(2,1)}, u32[]{:S(2)}, u32[]{:S(2)}) collective-permute-start(bf16[256,640]{1,0:T(8,128)(2,1)S(1)} %copy-done.12), channel_id=1, source_target_pairs={{65,0},{66,1},{67,2},{68,3},{69,4},{70,5},{71,6},{72,7},{73,8},{74... | collective-permute-start | bytes 983048 | tf_op jit(solution)/shard_map/ppermute | solution.py:16
  67.0 2.9 %fusion.7 = f32[10,64,512]{2,1,0:T(8,128)} fusion(bf16[512,10,64]{0,2,1:T(8,128)(2,1)S(1)} %bitcast.68, f32[10,512,512]{1,2,0:T(8,128)S(1)} %get-tuple-element.28, pred[512,512]{0,1:T(8,128)(4,1)S(1)} %fusion.23), kind=kOutput, calls=%fused_computation.8 | convolution fusion | flops 343408640 | bytes 12713984 | tf_op jit(solution)/shard_map/hqk,khd->qhd/dot_general | solution.py:37
  70.6 2.4 %pad_maximum_fusion.1 = bf16[1024,640]{1,0:T(8,128)(2,1)} fusion(bf16[256,640]{1,0:T(8,128)(2,1)} %collective-permute-done.7, bf16[256,640]{1,0:T(8,128)(2,1)} %collective-permute-done.6, bf16[256,640]{1,0:T(8,128)(2,1)} %collective-permute-done.5, bf16[256,640]{1,0:T(8,128)(2,1)S(1)} %collective-permute-done.4), kind=kLoop, calls=%fused_computation.26 | loop fusion | flops 5242880 | bytes 2621440 | tf_op jit(solution)/shard_map/concatenate | solution.py:119
  73.0 2.5 %copy.30 = bf16[1024,640]{0,1:T(8,128)(2,1)} copy(bf16[1024,640]{1,0:T(8,128)(2,1)} %pad_maximum_fusion.1) | data formatting | bytes 2621440 | tf_op jit(solution)/shard_map/concatenate | solution.py:119
  75.5 3.6 %collective-permute-done.2 = bf16[256,640]{1,0:T(8,128)(2,1)} collective-permute-done((bf16[256,640]{1,0:T(8,128)(2,1)S(1)}, bf16[256,640]{1,0:T(8,128)(2,1)}, u32[]{:S(2)}, u32[]{:S(2)}) %collective-permute-start.2) | collective-permute-done | bytes 327712 | tf_op jit(solution)/shard_map/ppermute | solution.py:16
  79.1 2.5 %pad_maximum_fusion = bf16[1024,640]{1,0:T(8,128)(2,1)} fusion(bf16[256,640]{1,0:T(8,128)(2,1)} %collective-permute-done.3, bf16[256,640]{1,0:T(8,128)(2,1)} %collective-permute-done.2, bf16[256,640]{1,0:T(8,128)(2,1)} %collective-permute-done.1, bf16[256,640]{1,0:T(8,128)(2,1)} %collective-permute-done), kind=kLoop, calls=%fused_computation.25 | loop fusion | flops 5242880 | bytes 2621440 | tf_op jit(solution)/shard_map/concatenate | solution.py:120
  81.6 2.6 %copy.29 = bf16[1024,640]{0,1:T(8,128)(2,1)} copy(bf16[1024,640]{1,0:T(8,128)(2,1)} %pad_maximum_fusion) | data formatting | bytes 2621440 | tf_op jit(solution)/shard_map/concatenate | solution.py:120
  84.2 10.9 %fusion = (f32[10,512]{1,0:T(8,128)S(1)}, f32[10,512,1024]{2,1,0:T(8,128)}) fusion(pred[1024]{0:T(1024)(128)(4,1)S(1)} %fusion.26, bf16[512,10,64]{0,2,1:T(8,128)(2,1)S(1)} %bitcast.72, bf16[1024,10,64]{0,2,1:T(8,128)(2,1)} %bitcast.69), kind=kOutput, calls=%fused_computation.1 | convolution fusion | flops 686812160 | bytes 22959104 | tf_op jit(solution)/shard_map/qhd,khd->hqk/dot_general | solution.py:32
  95.1 9.0 %divide_convert_fusion = bf16[512,10,64]{0,2,1:T(8,128)(2,1)S(1)} fusion(f32[10,64,512]{2,1,0:T(8,128)S(1)} %copy-done.6, bf16[1024,10,64]{0,2,1:T(8,128)(2,1)S(1)} %bitcast.70, f32[10,512,1024]{2,1,0:T(8,128)} %get-tuple-element.30, pred[1024]{0:T(1024)(128)(4,1)S(1)} %fusion.26, f32[512,10]{0,1:T(8,128)S(1)} %add_bitcast_fusion), kind=kOutput, calls=%fused_computation.27 | convolution fusion | flops 687800320 | bytes 24269824 | tf_op jit(solution)/shard_map/hqk,khd->qhd/dot_general | solution.py:37
  104.2 2.7 %fusion.39 = f32[512,1280]{1,0:T(8,128)} fusion(bf16[512,640]{0,1:T(8,128)(2,1)S(1)} %bitcast.74, bf16[640,1280]{1,0:T(8,128)(2,1)S(1)} %copy-done.18), kind=kOutput, calls=%fused_computation.72 | convolution fusion | flops 838860800 | bytes 4915200 | tf_op jit(solution)/shard_map/dot_general | solution.py:127
  106.9 0.0 all-reduce.2.cloned.1.call-update
  106.9 1.1 copy-done.5
  108.0 0.8 fusion.34
  108.8 0.3 collective-permute-start.10
  109.0 0.8 fusion.35
  109.8 3.1 %collective-permute-start.8 = (bf16[256,640]{1,0:T(8,128)(2,1)}, bf16[256,640]{1,0:T(8,128)(2,1)}, u32[]{:S(2)}, u32[]{:S(2)}) collective-permute-start(bf16[256,640]{1,0:T(8,128)(2,1)} %get-tuple-element.14), channel_id=1, source_target_pairs={{96,0},{97,1},{98,2},{99,3},{100,4},{101,5},{102,6},{103,7},{104,8... | collective-permute-start | bytes 983048 | tf_op jit(solution)/shard_map/ppermute | solution.py:16
  112.9 0.8 collective-permute-start.9
  113.7 0.7 fusion.36
  118.4 0.1 broadcast.150.clone.1
  118.4 1.0 bitcast_dynamic-update-slice_fusion.1
  119.5 2.1 %collective-permute-done.8 = bf16[256,640]{1,0:T(8,128)(2,1)} collective-permute-done((bf16[256,640]{1,0:T(8,128)(2,1)}, bf16[256,640]{1,0:T(8,128)(2,1)}, u32[]{:S(2)}, u32[]{:S(2)}) %collective-permute-start.8) | collective-permute-done | bytes 327712 | tf_op jit(solution)/shard_map/ppermute | solution.py:16
  121.6 0.1 broadcast.150.clone
  121.6 1.0 bitcast_dynamic-update-slice_fusion.3
  122.7 1.0 bitcast_dynamic-update-slice_fusion
  123.7 0.0 copy-start.13
  123.7 4.0 %collective-permute-done.9 = bf16[256,640]{1,0:T(8,128)(2,1)} collective-permute-done((bf16[256,640]{1,0:T(8,128)(2,1)S(1)}, bf16[256,640]{1,0:T(8,128)(2,1)}, u32[]{:S(2)}, u32[]{:S(2)}) %collective-permute-start.9) | collective-permute-done | bytes 327712 | tf_op jit(solution)/shard_map/ppermute | solution.py:16
  127.7 1.0 bitcast_dynamic-update-slice_fusion.2
  128.7 0.8 copy-done.10
  129.6 63.5 %all-reduce.2.cloned.1.call-done = f32[512,1280]{1,0:T(8,128)} async-done(((f32[512,1280]{1,0:T(8,128)}), f32[512,1280]{1,0:T(8,128)}) %all-reduce.2.cloned.1.call-update) | async-done | bytes 2621456 | tf_op jit(solution)/shard_map/psum | solution.py:128
  193.0 2.1 %multiply_reduce_fusion.1 = f32[512]{0:T(512)S(1)} fusion(f32[512,1280]{1,0:T(8,128)} %all-reduce.2.cloned.1.call-done), kind=kLoop, calls=%fused_computation.20 | loop fusion | flops 1310208 | bytes 2623488 | tf_op jit(solution)/shard_map/reduce_sum | solution.py:20
  195.2 0.4 copy-done.2
  195.6 0.8 multiply_reduce_fusion
  196.4 1.8 multiply_convert_fusion
  (50 shorter events, 0.2 us)
Async XLA Ops:
  7.2 30.0 %copy-start = (bf16[1280,640]{1,0:T(8,128)(2,1)S(1)}, bf16[1280,640]{1,0:T(8,128)(2,1)}, u32[]{:S(2)}) copy-start(bf16[1280,640]{1,0:T(8,128)(2,1)} %param.14) | copy-start | bytes 4915204
  7.2 185.9 %all-reduce.2.cloned.1.call-start = ((), (), s32[]{:S(2)}) async-start(), calls=%async_computation | async-start | bytes 5242880 | tf_op jit(solution)/shard_map/psum | solution.py:128
  16.5 14.2 %copy-start.8 = (bf16[4,256,640]{2,1,0:T(8,128)(2,1)S(1)}, bf16[4,256,640]{2,1,0:T(8,128)(2,1)}, u32[]{:S(2)}) copy-start(bf16[4,256,640]{2,1,0:T(8,128)(2,1)} %param.21) | copy-start | bytes 3932164
  19.0 13.5 %copy-start.3 = (bf16[512,1280]{1,0:T(8,128)(2,1)S(1)}, bf16[512,1280]{1,0:T(8,128)(2,1)}, u32[]{:S(2)}) copy-start(bf16[512,1280]{1,0:T(8,128)(2,1)} %param.13) | copy-start | bytes 3932164
  19.0 41.7 %collective-permute-start.4 = (bf16[256,640]{1,0:T(8,128)(2,1)}, bf16[256,640]{1,0:T(8,128)(2,1)S(1)}, u32[]{:S(2)}, u32[]{:S(2)}) collective-permute-start(bf16[256,640]{1,0:T(8,128)(2,1)} %get-tuple-element.3), channel_id=1, source_target_pairs={{1,0},{2,1},{3,2},{4,3},{5,4},{6,5},{7,6},{8,7},{9,8},{10,9},{11,1... | collective-permute-start | bytes 983048 | tf_op jit(solution)/shard_map/ppermute | solution.py:16
  22.3 41.3 %collective-permute-start.5 = (bf16[256,640]{1,0:T(8,128)(2,1)}, bf16[256,640]{1,0:T(8,128)(2,1)}, u32[]{:S(2)}, u32[]{:S(2)}) collective-permute-start(bf16[256,640]{1,0:T(8,128)(2,1)} %get-tuple-element.4), channel_id=1, source_target_pairs={{33,0},{34,1},{35,2},{36,3},{37,4},{38,5},{39,6},{40,7},{41,8},{42... | collective-permute-start | bytes 983048 | tf_op jit(solution)/shard_map/ppermute | solution.py:16
  29.5 34.9 %collective-permute-start.7 = (bf16[256,640]{1,0:T(8,128)(2,1)}, bf16[256,640]{1,0:T(8,128)(2,1)}, u32[]{:S(2)}, u32[]{:S(2)}) collective-permute-start(bf16[256,640]{1,0:T(8,128)(2,1)} %get-tuple-element.5), channel_id=1, source_target_pairs={{97,0},{98,1},{99,2},{100,3},{101,4},{102,5},{103,6},{104,7},{105,... | collective-permute-start | bytes 983048 | tf_op jit(solution)/shard_map/ppermute | solution.py:16
  30.4 2.6 %copy-start.17 = (bf16[1280,640]{1,0:T(8,128)(2,1)S(1)}, bf16[1280,640]{1,0:T(8,128)(2,1)}, u32[]{:S(2)}) copy-start(bf16[1280,640]{1,0:T(8,128)(2,1)} %param.16) | copy-start | bytes 4915204
  30.4 40.2 %collective-permute-start.6 = (bf16[256,640]{1,0:T(8,128)(2,1)}, bf16[256,640]{1,0:T(8,128)(2,1)}, u32[]{:S(2)}, u32[]{:S(2)}) collective-permute-start(bf16[256,640]{1,0:T(8,128)(2,1)} %get-tuple-element.6), channel_id=1, source_target_pairs={{65,0},{66,1},{67,2},{68,3},{69,4},{70,5},{71,6},{72,7},{73,8},{74... | collective-permute-start | bytes 983048 | tf_op jit(solution)/shard_map/ppermute | solution.py:16
  31.8 43.7 %collective-permute-start = (bf16[256,640]{1,0:T(8,128)(2,1)}, bf16[256,640]{1,0:T(8,128)(2,1)}, u32[]{:S(2)}, u32[]{:S(2)}) collective-permute-start(bf16[256,640]{1,0:T(8,128)(2,1)} %get-tuple-element.7), channel_id=1, source_target_pairs={{1,0},{2,1},{3,2},{4,3},{5,4},{6,5},{7,6},{8,7},{9,8},{10,9},{11,1... | collective-permute-start | bytes 983048 | tf_op jit(solution)/shard_map/ppermute | solution.py:16
  49.6 1.5 copy-start.15
  56.0 8.3 %copy-start.12 = (bf16[256,640]{1,0:T(8,128)(2,1)S(1)}, bf16[256,640]{1,0:T(8,128)(2,1)}, u32[]{:S(2)}) copy-start(bf16[256,640]{1,0:T(8,128)(2,1)} %get-tuple-element.10) | copy-start | bytes 983044
  56.0 11.0 %copy-start.4 = (bf16[512,640]{0,1:T(8,128)(2,1)S(1)}, bf16[512,640]{0,1:T(8,128)(2,1)}, u32[]{:S(2)}) copy-start(bf16[512,640]{0,1:T(8,128)(2,1)} %copy.21) | copy-start | bytes 1966084
  60.7 14.7 %collective-permute-start.1 = (bf16[256,640]{1,0:T(8,128)(2,1)}, bf16[256,640]{1,0:T(8,128)(2,1)}, u32[]{:S(2)}, u32[]{:S(2)}) collective-permute-start(bf16[256,640]{1,0:T(8,128)(2,1)} %get-tuple-element.8), channel_id=1, source_target_pairs={{33,0},{34,1},{35,2},{36,3},{37,4},{38,5},{39,6},{40,7},{41,8},{42... | collective-permute-start | bytes 983048 | tf_op jit(solution)/shard_map/ppermute | solution.py:16
  63.6 11.9 %collective-permute-start.3 = (bf16[256,640]{1,0:T(8,128)(2,1)}, bf16[256,640]{1,0:T(8,128)(2,1)}, u32[]{:S(2)}, u32[]{:S(2)}) collective-permute-start(bf16[256,640]{1,0:T(8,128)(2,1)} %get-tuple-element.9), channel_id=1, source_target_pairs={{97,0},{98,1},{99,2},{100,3},{101,4},{102,5},{103,6},{104,7},{105,... | collective-permute-start | bytes 983048 | tf_op jit(solution)/shard_map/ppermute | solution.py:16
  64.4 14.8 %collective-permute-start.2 = (bf16[256,640]{1,0:T(8,128)(2,1)S(1)}, bf16[256,640]{1,0:T(8,128)(2,1)}, u32[]{:S(2)}, u32[]{:S(2)}) collective-permute-start(bf16[256,640]{1,0:T(8,128)(2,1)S(1)} %copy-done.12), channel_id=1, source_target_pairs={{65,0},{66,1},{67,2},{68,3},{69,4},{70,5},{71,6},{72,7},{73,8},{74... | collective-permute-start | bytes 983048 | tf_op jit(solution)/shard_map/ppermute | solution.py:16
  81.6 2.6 %copy-start.9 = (bf16[512,640]{0,1:T(8,128)(2,1)S(1)}, bf16[512,640]{0,1:T(8,128)(2,1)}, u32[]{:S(2)}) copy-start(bf16[512,640]{0,1:T(8,128)(2,1)} %copy.24) | copy-start | bytes 1966084
  84.2 10.9 %copy-start.14 = (f32[10,512]{1,0:T(8,128)S(1)}, f32[10,512]{1,0:T(8,128)}, u32[]{:S(2)}) copy-start(f32[10,512]{1,0:T(8,128)} %get-tuple-element.27) | copy-start | bytes 61444
  84.2 11.0 %copy-start.6 = (f32[10,64,512]{2,1,0:T(8,128)S(1)}, f32[10,64,512]{2,1,0:T(8,128)}, u32[]{:S(2)}) copy-start(f32[10,64,512]{2,1,0:T(8,128)} %fusion.7) | copy-start | bytes 3932164
  84.2 11.0 %copy-start.7 = (bf16[1024,640]{0,1:T(8,128)(2,1)S(1)}, bf16[1024,640]{0,1:T(8,128)(2,1)}, u32[]{:S(2)}) copy-start(bf16[1024,640]{0,1:T(8,128)(2,1)} %copy.29) | copy-start | bytes 3932164
  95.1 9.0 %copy-start.18 = (bf16[640,1280]{1,0:T(8,128)(2,1)S(1)}, bf16[640,1280]{1,0:T(8,128)(2,1)}, u32[]{:S(2)}) copy-start(bf16[640,1280]{1,0:T(8,128)(2,1)} %param.17) | copy-start | bytes 4915204
  106.9 1.1 copy-start.5
  108.0 5.7 %copy-start.16 = (s32[256]{0:T(256)S(1)}, s32[256]{0:T(256)}, u32[]{:S(2)}) copy-start(s32[256]{0:T(256)} %param.25) | copy-start | bytes 3076
  108.8 9.6 %collective-permute-start.10 = (bf16[256,640]{1,0:T(8,128)(2,1)}, bf16[256,640]{1,0:T(8,128)(2,1)}, u32[]{:S(2)}, u32[]{:S(2)}) collective-permute-start(bf16[256,640]{1,0:T(8,128)(2,1)} %get-tuple-element.12), channel_id=1, source_target_pairs={{96,0},{97,1},{98,2},{99,3},{100,4},{101,5},{102,6},{103,7},{104,8... | collective-permute-start | bytes 983048 | tf_op jit(solution)/shard_map/ppermute | solution.py:16
  109.8 11.8 %collective-permute-start.8 = (bf16[256,640]{1,0:T(8,128)(2,1)}, bf16[256,640]{1,0:T(8,128)(2,1)}, u32[]{:S(2)}, u32[]{:S(2)}) collective-permute-start(bf16[256,640]{1,0:T(8,128)(2,1)} %get-tuple-element.14), channel_id=1, source_target_pairs={{96,0},{97,1},{98,2},{99,3},{100,4},{101,5},{102,6},{103,7},{104,8... | collective-permute-start | bytes 983048 | tf_op jit(solution)/shard_map/ppermute | solution.py:16
  112.9 9.8 %collective-permute-start.11 = (bf16[256,640]{1,0:T(8,128)(2,1)S(1)}, bf16[256,640]{1,0:T(8,128)(2,1)}, u32[]{:S(2)}, u32[]{:S(2)}) collective-permute-start(bf16[256,640]{1,0:T(8,128)(2,1)S(1)} %get-tuple-element.11), channel_id=1, source_target_pairs={{32,0},{33,1},{34,2},{35,3},{36,4},{37,5},{38,6},{39,7},{40,8},{41... | collective-permute-start | bytes 983048 | tf_op jit(solution)/shard_map/ppermute | solution.py:16
  112.9 14.8 %collective-permute-start.9 = (bf16[256,640]{1,0:T(8,128)(2,1)S(1)}, bf16[256,640]{1,0:T(8,128)(2,1)}, u32[]{:S(2)}, u32[]{:S(2)}) collective-permute-start(bf16[256,640]{1,0:T(8,128)(2,1)S(1)} %get-tuple-element.13), channel_id=1, source_target_pairs={{32,0},{33,1},{34,2},{35,3},{36,4},{37,5},{38,6},{39,7},{40,8},{41... | collective-permute-start | bytes 983048 | tf_op jit(solution)/shard_map/ppermute | solution.py:16
  123.7 71.5 %copy-start.11 = (bf16[2,256,640]{2,1,0:T(8,128)(2,1)}, bf16[2,256,640]{2,1,0:T(8,128)(2,1)S(1)}, u32[]{:S(2)}) copy-start(bf16[2,256,640]{2,1,0:T(8,128)(2,1)S(1)} %bitcast_dynamic-update-slice_fusion) | copy-start | bytes 1966084
  123.7 71.5 %copy-start.13 = (f32[1280]{0:T(1024)S(1)}, f32[1280]{0:T(1024)}, u32[]{:S(2)}) copy-start(f32[1280]{0:T(1024)} %param.19) | copy-start | bytes 15364
  128.7 0.8 copy-start.10
  193.0 2.5 %copy-start.2 = (f32[512,1280]{1,0:T(8,128)S(1)}, f32[512,1280]{1,0:T(8,128)}, u32[]{:S(2)}) copy-start(f32[512,1280]{1,0:T(8,128)} %all-reduce.2.cloned.1.call-done) | copy-start | bytes 7864324
  196.4 1.8 copy-start.1
Sparse Core Ops, SparseCore 0:
  107.0 85.9 all-reduce.1
where the time goes:
time: 206 us; the launch traced here: 205 us
  waiting for transfers between devices  73.2 us (36%)
  matrix products  39.1 us (19%)
  local copies, waits for them, and re-layouts  29.9 us (15%)
  between operations  27.5 us (13%)
  starting transfers between devices  22.1 us (11%)
  other arithmetic  13.2 us (6%)
    psum x1, waiting for transfers between devices, body(): branch = lax.psum(partial_branch, 'kv')  63.5 us
    ppermute x12, starting transfers between devices, from_behind(): return lax.ppermute(block, axis, route)  22.1 us
    dot_general x2, matrix products, attend(): jnp.einsum('qhd,khd->hqk', query_heads, key_heads, preferred_element_type...  15.6 us
    dot_general x2, matrix products, attend(): jnp.einsum('hqk,khd->qhd', weights.astype(jnp.bfloat16), value_heads, pre...  11.9 us
    ppermute x12, waiting for transfers between devices, from_behind(): return lax.ppermute(block, axis, route)  9.72 us
  transfers between devices with their start and end apart: 13, of which 4 were waited for; matrix products, arithmetic and copies ran while one was open for 21% of the time, Pallas kernels for 0%

commit v1 on v0

--- a/solution.py
+++ b/solution.py
@@ -125,7 +125,7 @@
     mixed = mixed + more_mixed
     attended = (mixed / totals.T[:, :, None]).astype(jnp.bfloat16).reshape(tokens_here, width_half)
     partial_branch = jnp.dot(attended, w_out, preferred_element_type=jnp.float32)
-    branch = lax.psum(partial_branch, "kv")
+    branch = jnp.sum(lax.all_gather(partial_branch, "kv"), axis=0)
     updated = anchor + eigen_rate * (rms_scale(branch) - anchor)
     layer_out = rms_scale(updated).astype(jnp.bfloat16)
     new_keys, new_values = relay(key_rows, value_rows, placement)

time: 206 us -> 198 us (0.961)
  waiting for transfers between devices: 73.2 us -> 62 us
  other arithmetic: 13.2 us -> 17.8 us
    psum x1 -> x0, waiting for transfers between devices: 63.5 us -> none  [body(): branch = lax.psum(partial_branch, 'kv')]
    all_gather x0 -> x1, waiting for transfers between devices: none -> 52 us  [body(): branch = jnp.sum(lax.all_gather(partial_branch, 'kv'), axis=0)]
    reduce_sum x0 -> x1, other arithmetic: none -> 4.59 us  [body(): branch = jnp.sum(lax.all_gather(partial_branch, 'kv'), axis=0)]
  transfers between devices with their start and end apart: 13 -> 13, of which waited for: 4 -> 4; matrix products, arithmetic and copies ran while one was open for 21% -> 22% of each run, Pallas kernels for 0% -> 0%
where the time goes in v1:
time: 198 us; the launch traced here: 197 us
  waiting for transfers between devices  62 us (31%)
  matrix products  39 us (20%)
  local copies, waits for them, and re-layouts  29.1 us (15%)
  between operations  27.2 us (14%)
  starting transfers between devices  22.1 us (11%)
  other arithmetic  17.8 us (9%)
    all_gather x1, waiting for transfers between devices, body(): branch = jnp.sum(lax.all_gather(partial_branch, 'kv'), axis=0)  52 us
    ppermute x12, starting transfers between devices, from_behind(): return lax.ppermute(block, axis, route)  22.1 us
    dot_general x2, matrix products, attend(): jnp.einsum('qhd,khd->hqk', query_heads, key_heads, preferred_element_type...  15.6 us
    dot_general x2, matrix products, attend(): jnp.einsum('hqk,khd->qhd', weights.astype(jnp.bfloat16), value_heads, pre...  11.9 us
    ppermute x12, waiting for transfers between devices, from_behind(): return lax.ppermute(block, axis, route)  10 us
    reduce_sum x1, other arithmetic, body(): branch = jnp.sum(lax.all_gather(partial_branch, 'kv'), axis=0)  4.59 us
    dot_general x1, matrix products, body(): jnp.dot(hidden_in, w_key, preferred_element_type=jnp.float32)  4.1 us
  transfers between devices with their start and end apart: 13, of which 4 were waited for; matrix products, arithmetic and copies ran while one was open for 22% of the time, Pallas kernels for 0%

profile of v1, /device:TPU:1, one launch (start us, length us, event | category | flops | bytes accessed | tf_op | source)
XLA Modules:
  0.0 197.2 jit_solution(13607699880387781058)
XLA Ops:
  7.2 0.0 copy-start
  7.2 0.0 all-gather.3.cloned.1.call-start
  7.3 1.4 constant_dynamic-slice_fusion
  16.5 0.0 copy-start.8
  16.5 2.5 %dynamic-slice_bitcast_fusion.3 = (bf16[256,640]{1,0:T(8,128)(2,1)}, bf16[256,640]{1,0:T(8,128)(2,1)}, bf16[256,640]{1,0:T(8,128)(2,1)}, bf16[256,640]{1,0:T(8,128)(2,1)}) fusion(bf16[4,256,640]{2,1,0:T(8,128)(2,1)} %param.20, s32[]{:T(128)S(6)} %select_n.116, s32[]{:T(128)S(6)} %select_n.120, s32[]{:T(128)S(6)} %select_n.128, s32[]{:T(128)S(6)} %select_n.124), kind=kLoop, calls=%fused_computation.39 | loop fusion | bytes 2621456 | tf_op jit(solution)/shard_map/jit(dynamic_index_in_dim)/squeeze | solution.py:52
  19.0 3.2 %collective-permute-start.4 = (bf16[256,640]{1,0:T(8,128)(2,1)}, bf16[256,640]{1,0:T(8,128)(2,1)S(1)}, u32[]{:S(2)}, u32[]{:S(2)}) collective-permute-start(bf16[256,640]{1,0:T(8,128)(2,1)} %get-tuple-element.3), channel_id=1, source_target_pairs={{1,0},{2,1},{3,2},{4,3},{5,4},{6,5},{7,6},{8,7},{9,8},{10,9},{11,1... | collective-permute-start | bytes 983048 | tf_op jit(solution)/shard_map/ppermute | solution.py:16
  22.3 7.2 %collective-permute-start.5 = (bf16[256,640]{1,0:T(8,128)(2,1)}, bf16[256,640]{1,0:T(8,128)(2,1)}, u32[]{:S(2)}, u32[]{:S(2)}) collective-permute-start(bf16[256,640]{1,0:T(8,128)(2,1)} %get-tuple-element.4), channel_id=1, source_target_pairs={{33,0},{34,1},{35,2},{36,3},{37,4},{38,5},{39,6},{40,7},{41,8},{42... | collective-permute-start | bytes 983048 | tf_op jit(solution)/shard_map/ppermute | solution.py:16
  29.5 0.7 collective-permute-start.7
  30.2 0.6 collective-permute-start.6
  30.7 1.1 dynamic-slice_bitcast_fusion.7
  32.5 0.3 fusion.15
  32.9 0.1 fusion.23
  33.0 2.0 %fusion.22 = bf16[512,640]{1,0:T(8,128)(2,1)} fusion(bf16[512,1280]{1,0:T(8,128)(2,1)S(1)} %copy-done.3, bf16[1280,640]{1,0:T(8,128)(2,1)S(1)} %copy-done.17, f32[512]{0:T(512)S(1)} %add_rsqrt_fusion.4), kind=kOutput, calls=%fused_computation.24 | convolution fusion | flops 839516160 | bytes 3606528 | tf_op jit(solution)/shard_map/dot_general | solution.py:104
  35.0 2.2 %copy.21 = bf16[512,640]{0,1:T(8,128)(2,1)} copy(bf16[512,640]{1,0:T(8,128)(2,1)} %fusion.22) | data formatting | bytes 1310720 | tf_op jit(solution)/shard_map/convert_element_type | solution.py:105
  37.2 2.7 %fusion.38 = (f32[512,640]{1,0:T(8,128)}, f32[512,640]{1,0:T(8,128)}) fusion(bf16[512,1280]{1,0:T(8,128)(2,1)S(1)} %copy-done.3, bf16[1280,640]{1,0:T(8,128)(2,1)S(1)} %copy-done), kind=kOutput, calls=%fused_computation.71 | convolution fusion | flops 839188480 | bytes 5570560 | tf_op jit(solution)/shard_map/dot_general | solution.py:100
  39.9 1.7 copy.22
  41.6 0.2 reduce_sum.73
  41.8 0.1 mul.111
  41.9 1.5 copy.23
  43.4 4.1 %fusion.37 = (f32[512,640]{1,0:T(8,128)}, f32[512,640]{1,0:T(8,128)}) fusion(bf16[512,1280]{1,0:T(8,128)(2,1)S(1)} %copy-done.3, bf16[1280,640]{1,0:T(8,128)(2,1)} %param.15), kind=kOutput, calls=%fused_computation.70 | convolution fusion | flops 839188480 | bytes 5570560 | tf_op jit(solution)/shard_map/dot_general | solution.py:102
  47.5 1.7 copy.25
  49.2 0.2 reduce_sum.74
  49.4 0.1 mul.118
  49.6 0.0 copy-start.15
  49.6 1.5 copy.26
  51.0 2.8 %multiply_convert_fusion.1 = (bf16[512,640]{1,0:T(8,128)(2,1)S(1)}, bf16[512,640]{1,0:T(8,128)(2,1)S(1)}) fusion(f32[512,640]{1,0:T(8,128)} %get-tuple-element.24, f32[512,640]{1,0:T(8,128)} %copy.26, f32[640]{0:T(1024)S(1)} %copy-done.15, f32[512,640]{1,0:T(8,128)} %get-tuple-element.26, f32[512,640]{1,0:T(8,128)} %copy.23), kind=kLoop, calls=%fused_computation.28 | loop fusion | flops 1966080 | bytes 6556160 | tf_op jit(solution)/shard_map/convert_element_type | solution.py:26
  53.8 1.1 copy.24
  54.9 1.1 copy.27
  56.0 4.7 %fusion.5 = (f32[10,512]{1,0:T(8,128)}, f32[10,512,512]{1,2,0:T(8,128)S(1)}) fusion(pred[512,512]{0,1:T(8,128)(4,1)S(1)} %fusion.23, bf16[512,10,64]{0,2,1:T(8,128)(2,1)} %bitcast.73, bf16[512,10,64]{0,2,1:T(8,128)(2,1)} %bitcast.75), kind=kOutput, calls=%fused_computation.6 | convolution fusion | flops 343403520 | bytes 12079104 | tf_op jit(solution)/shard_map/qhd,khd->hqk/dot_general | solution.py:32
  60.7 2.8 %collective-permute-start.1 = (bf16[256,640]{1,0:T(8,128)(2,1)}, bf16[256,640]{1,0:T(8,128)(2,1)}, u32[]{:S(2)}, u32[]{:S(2)}) collective-permute-start(bf16[256,640]{1,0:T(8,128)(2,1)} %get-tuple-element.8), channel_id=1, source_target_pairs={{33,0},{34,1},{35,2},{36,3},{37,4},{38,5},{39,6},{40,7},{41,8},{42... | collective-permute-start | bytes 983048 | tf_op jit(solution)/shard_map/ppermute | solution.py:16
  63.6 0.8 collective-permute-start.3
  64.4 2.7 %collective-permute-start.2 = (bf16[256,640]{1,0:T(8,128)(2,1)S(1)}, bf16[256,640]{1,0:T(8,128)(2,1)}, u32[]{:S(2)}, u32[]{:S(2)}) collective-permute-start(bf16[256,640]{1,0:T(8,128)(2,1)S(1)} %copy-done.12), channel_id=1, source_target_pairs={{65,0},{66,1},{67,2},{68,3},{69,4},{70,5},{71,6},{72,7},{73,8},{74... | collective-permute-start | bytes 983048 | tf_op jit(solution)/shard_map/ppermute | solution.py:16
  67.0 2.9 %fusion.7 = f32[10,64,512]{2,1,0:T(8,128)} fusion(bf16[512,10,64]{0,2,1:T(8,128)(2,1)S(1)} %bitcast.70, f32[10,512,512]{1,2,0:T(8,128)S(1)} %get-tuple-element.28, pred[512,512]{0,1:T(8,128)(4,1)S(1)} %fusion.23), kind=kOutput, calls=%fused_computation.8 | convolution fusion | flops 343408640 | bytes 12713984 | tf_op jit(solution)/shard_map/hqk,khd->qhd/dot_general | solution.py:37
  70.6 2.4 %pad_maximum_fusion.1 = bf16[1024,640]{1,0:T(8,128)(2,1)} fusion(bf16[256,640]{1,0:T(8,128)(2,1)} %collective-permute-done.7, bf16[256,640]{1,0:T(8,128)(2,1)} %collective-permute-done.6, bf16[256,640]{1,0:T(8,128)(2,1)} %collective-permute-done.5, bf16[256,640]{1,0:T(8,128)(2,1)S(1)} %collective-permute-done.4), kind=kLoop, calls=%fused_computation.26 | loop fusion | flops 5242880 | bytes 2621440 | tf_op jit(solution)/shard_map/concatenate | solution.py:119
  73.0 2.5 %copy.30 = bf16[1024,640]{0,1:T(8,128)(2,1)} copy(bf16[1024,640]{1,0:T(8,128)(2,1)} %pad_maximum_fusion.1) | data formatting | bytes 2621440 | tf_op jit(solution)/shard_map/concatenate | solution.py:119
  75.5 3.6 %collective-permute-done.2 = bf16[256,640]{1,0:T(8,128)(2,1)} collective-permute-done((bf16[256,640]{1,0:T(8,128)(2,1)S(1)}, bf16[256,640]{1,0:T(8,128)(2,1)}, u32[]{:S(2)}, u32[]{:S(2)}) %collective-permute-start.2) | collective-permute-done | bytes 327712 | tf_op jit(solution)/shard_map/ppermute | solution.py:16
  79.1 2.5 %pad_maximum_fusion = bf16[1024,640]{1,0:T(8,128)(2,1)} fusion(bf16[256,640]{1,0:T(8,128)(2,1)} %collective-permute-done.3, bf16[256,640]{1,0:T(8,128)(2,1)} %collective-permute-done.2, bf16[256,640]{1,0:T(8,128)(2,1)} %collective-permute-done.1, bf16[256,640]{1,0:T(8,128)(2,1)} %collective-permute-done), kind=kLoop, calls=%fused_computation.25 | loop fusion | flops 5242880 | bytes 2621440 | tf_op jit(solution)/shard_map/concatenate | solution.py:120
  81.6 2.6 %copy.29 = bf16[1024,640]{0,1:T(8,128)(2,1)} copy(bf16[1024,640]{1,0:T(8,128)(2,1)} %pad_maximum_fusion) | data formatting | bytes 2621440 | tf_op jit(solution)/shard_map/concatenate | solution.py:120
  84.2 10.9 %fusion = (f32[10,512]{1,0:T(8,128)S(1)}, f32[10,512,1024]{2,1,0:T(8,128)}) fusion(pred[1024]{0:T(1024)(128)(4,1)S(1)} %fusion.26, bf16[512,10,64]{0,2,1:T(8,128)(2,1)S(1)} %bitcast.74, bf16[1024,10,64]{0,2,1:T(8,128)(2,1)} %bitcast.71), kind=kOutput, calls=%fused_computation.1 | convolution fusion | flops 686812160 | bytes 22959104 | tf_op jit(solution)/shard_map/qhd,khd->hqk/dot_general | solution.py:32
  95.1 9.0 %divide_convert_fusion = bf16[512,10,64]{0,2,1:T(8,128)(2,1)S(1)} fusion(f32[10,64,512]{2,1,0:T(8,128)S(1)} %copy-done.6, bf16[1024,10,64]{0,2,1:T(8,128)(2,1)S(1)} %bitcast.72, f32[10,512,1024]{2,1,0:T(8,128)} %get-tuple-element.30, pred[1024]{0:T(1024)(128)(4,1)S(1)} %fusion.26, f32[512,10]{0,1:T(8,128)S(1)} %add_bitcast_fusion), kind=kOutput, calls=%fused_computation.27 | convolution fusion | flops 687800320 | bytes 24269824 | tf_op jit(solution)/shard_map/hqk,khd->qhd/dot_general | solution.py:37
  104.2 2.7 %fusion.39 = f32[512,1280]{1,0:T(8,128)} fusion(bf16[512,640]{0,1:T(8,128)(2,1)S(1)} %bitcast.76, bf16[640,1280]{1,0:T(8,128)(2,1)S(1)} %copy-done.18), kind=kOutput, calls=%fused_computation.72 | convolution fusion | flops 838860800 | bytes 4915200 | tf_op jit(solution)/shard_map/dot_general | solution.py:127
  106.8 0.0 all-gather.3.cloned.1.call-update
  106.9 1.1 copy-done.5
  107.9 0.8 fusion.34
  108.7 0.3 collective-permute-start.10
  109.0 0.8 fusion.35
  109.8 3.1 %collective-permute-start.8 = (bf16[256,640]{1,0:T(8,128)(2,1)}, bf16[256,640]{1,0:T(8,128)(2,1)}, u32[]{:S(2)}, u32[]{:S(2)}) collective-permute-start(bf16[256,640]{1,0:T(8,128)(2,1)} %get-tuple-element.14), channel_id=1, source_target_pairs={{96,0},{97,1},{98,2},{99,3},{100,4},{101,5},{102,6},{103,7},{104,8... | collective-permute-start | bytes 983048 | tf_op jit(solution)/shard_map/ppermute | solution.py:16
  112.8 0.8 collective-permute-start.9
  113.6 0.6 fusion.36
  117.9 0.1 broadcast.150.clone.1
  118.0 1.1 bitcast_dynamic-update-slice_fusion.1
  119.1 2.5 %collective-permute-done.8 = bf16[256,640]{1,0:T(8,128)(2,1)} collective-permute-done((bf16[256,640]{1,0:T(8,128)(2,1)}, bf16[256,640]{1,0:T(8,128)(2,1)}, u32[]{:S(2)}, u32[]{:S(2)}) %collective-permute-start.8) | collective-permute-done | bytes 327712 | tf_op jit(solution)/shard_map/ppermute | solution.py:16
  121.6 0.1 broadcast.150.clone
  121.6 1.0 bitcast_dynamic-update-slice_fusion.3
  122.7 1.0 bitcast_dynamic-update-slice_fusion
  123.7 0.0 copy-start.11
  123.7 3.9 %collective-permute-done.9 = bf16[256,640]{1,0:T(8,128)(2,1)} collective-permute-done((bf16[256,640]{1,0:T(8,128)(2,1)S(1)}, bf16[256,640]{1,0:T(8,128)(2,1)}, u32[]{:S(2)}, u32[]{:S(2)}) %collective-permute-start.9) | collective-permute-done | bytes 327712 | tf_op jit(solution)/shard_map/ppermute | solution.py:16
  127.6 1.0 bitcast_dynamic-update-slice_fusion.2
  128.6 52.0 %all-gather.3.cloned.1.call-done = f32[1024,1280]{1,0:T(8,128)} async-done(((f32[512,1280]{1,0:T(8,128)}), f32[1024,1280]{1,0:T(8,128)}) %all-gather.3.cloned.1.call-update) | async-done | bytes 5242896 | tf_op jit(solution)/shard_map/all_gather | solution.py:128
  180.6 4.6 %reduce_sum.77 = f32[512,1280]{1,0:T(8,128)} reduce(f32[2,512,1280]{2,1,0:T(8,128)} %bitcast.69, f32[]{:T(128)} %constant.136.clone.1), dimensions={0}, to_apply=%region_5.6 | reduce | flops 655360 | bytes 7864324 | tf_op jit(solution)/shard_map/reduce_sum | solution.py:128
  185.2 2.1 %multiply_reduce_fusion.1 = f32[512]{0:T(512)S(1)} fusion(f32[512,1280]{1,0:T(8,128)} %reduce_sum.77), kind=kLoop, calls=%fused_computation.20 | loop fusion | flops 1310208 | bytes 2623488 | tf_op jit(solution)/shard_map/reduce_sum | solution.py:20
  187.4 0.4 copy-done.2
  187.7 0.8 multiply_reduce_fusion
  188.6 1.8 multiply_convert_fusion
  (51 shorter events, 0.2 us)
Async XLA Ops:
  7.2 30.0 %copy-start = (bf16[1280,640]{1,0:T(8,128)(2,1)S(1)}, bf16[1280,640]{1,0:T(8,128)(2,1)}, u32[]{:S(2)}) copy-start(bf16[1280,640]{1,0:T(8,128)(2,1)} %param.14) | copy-start | bytes 4915204
  7.2 173.4 %all-gather.3.cloned.1.call-start = ((), (), s32[]{:S(2)}) async-start(), calls=%async_computation | async-start | bytes 7864320 | tf_op jit(solution)/shard_map/all_gather | solution.py:128
  16.5 14.2 %copy-start.8 = (bf16[4,256,640]{2,1,0:T(8,128)(2,1)S(1)}, bf16[4,256,640]{2,1,0:T(8,128)(2,1)}, u32[]{:S(2)}) copy-start(bf16[4,256,640]{2,1,0:T(8,128)(2,1)} %param.21) | copy-start | bytes 3932164
  19.0 13.5 %copy-start.3 = (bf16[512,1280]{1,0:T(8,128)(2,1)S(1)}, bf16[512,1280]{1,0:T(8,128)(2,1)}, u32[]{:S(2)}) copy-start(bf16[512,1280]{1,0:T(8,128)(2,1)} %param.13) | copy-start | bytes 3932164
  19.0 41.7 %collective-permute-start.4 = (bf16[256,640]{1,0:T(8,128)(2,1)}, bf16[256,640]{1,0:T(8,128)(2,1)S(1)}, u32[]{:S(2)}, u32[]{:S(2)}) collective-permute-start(bf16[256,640]{1,0:T(8,128)(2,1)} %get-tuple-element.3), channel_id=1, source_target_pairs={{1,0},{2,1},{3,2},{4,3},{5,4},{6,5},{7,6},{8,7},{9,8},{10,9},{11,1... | collective-permute-start | bytes 983048 | tf_op jit(solution)/shard_map/ppermute | solution.py:16
  22.3 41.3 %collective-permute-start.5 = (bf16[256,640]{1,0:T(8,128)(2,1)}, bf16[256,640]{1,0:T(8,128)(2,1)}, u32[]{:S(2)}, u32[]{:S(2)}) collective-permute-start(bf16[256,640]{1,0:T(8,128)(2,1)} %get-tuple-element.4), channel_id=1, source_target_pairs={{33,0},{34,1},{35,2},{36,3},{37,4},{38,5},{39,6},{40,7},{41,8},{42... | collective-permute-start | bytes 983048 | tf_op jit(solution)/shard_map/ppermute | solution.py:16
  29.5 34.9 %collective-permute-start.7 = (bf16[256,640]{1,0:T(8,128)(2,1)}, bf16[256,640]{1,0:T(8,128)(2,1)}, u32[]{:S(2)}, u32[]{:S(2)}) collective-permute-start(bf16[256,640]{1,0:T(8,128)(2,1)} %get-tuple-element.5), channel_id=1, source_target_pairs={{97,0},{98,1},{99,2},{100,3},{101,4},{102,5},{103,6},{104,7},{105,... | collective-permute-start | bytes 983048 | tf_op jit(solution)/shard_map/ppermute | solution.py:16
  30.2 2.8 %copy-start.17 = (bf16[1280,640]{1,0:T(8,128)(2,1)S(1)}, bf16[1280,640]{1,0:T(8,128)(2,1)}, u32[]{:S(2)}) copy-start(bf16[1280,640]{1,0:T(8,128)(2,1)} %param.16) | copy-start | bytes 4915204
  30.2 40.4 %collective-permute-start.6 = (bf16[256,640]{1,0:T(8,128)(2,1)}, bf16[256,640]{1,0:T(8,128)(2,1)}, u32[]{:S(2)}, u32[]{:S(2)}) collective-permute-start(bf16[256,640]{1,0:T(8,128)(2,1)} %get-tuple-element.6), channel_id=1, source_target_pairs={{65,0},{66,1},{67,2},{68,3},{69,4},{70,5},{71,6},{72,7},{73,8},{74... | collective-permute-start | bytes 983048 | tf_op jit(solution)/shard_map/ppermute | solution.py:16
  31.8 43.7 %collective-permute-start = (bf16[256,640]{1,0:T(8,128)(2,1)}, bf16[256,640]{1,0:T(8,128)(2,1)}, u32[]{:S(2)}, u32[]{:S(2)}) collective-permute-start(bf16[256,640]{1,0:T(8,128)(2,1)} %get-tuple-element.7), channel_id=1, source_target_pairs={{1,0},{2,1},{3,2},{4,3},{5,4},{6,5},{7,6},{8,7},{9,8},{10,9},{11,1... | collective-permute-start | bytes 983048 | tf_op jit(solution)/shard_map/ppermute | solution.py:16
  49.6 1.5 copy-start.15
  56.0 8.3 %copy-start.12 = (bf16[256,640]{1,0:T(8,128)(2,1)S(1)}, bf16[256,640]{1,0:T(8,128)(2,1)}, u32[]{:S(2)}) copy-start(bf16[256,640]{1,0:T(8,128)(2,1)} %get-tuple-element.10) | copy-start | bytes 983044
  56.0 11.0 %copy-start.4 = (bf16[512,640]{0,1:T(8,128)(2,1)S(1)}, bf16[512,640]{0,1:T(8,128)(2,1)}, u32[]{:S(2)}) copy-start(bf16[512,640]{0,1:T(8,128)(2,1)} %copy.21) | copy-start | bytes 1966084
  60.7 14.7 %collective-permute-start.1 = (bf16[256,640]{1,0:T(8,128)(2,1)}, bf16[256,640]{1,0:T(8,128)(2,1)}, u32[]{:S(2)}, u32[]{:S(2)}) collective-permute-start(bf16[256,640]{1,0:T(8,128)(2,1)} %get-tuple-element.8), channel_id=1, source_target_pairs={{33,0},{34,1},{35,2},{36,3},{37,4},{38,5},{39,6},{40,7},{41,8},{42... | collective-permute-start | bytes 983048 | tf_op jit(solution)/shard_map/ppermute | solution.py:16
  63.6 11.9 %collective-permute-start.3 = (bf16[256,640]{1,0:T(8,128)(2,1)}, bf16[256,640]{1,0:T(8,128)(2,1)}, u32[]{:S(2)}, u32[]{:S(2)}) collective-permute-start(bf16[256,640]{1,0:T(8,128)(2,1)} %get-tuple-element.9), channel_id=1, source_target_pairs={{97,0},{98,1},{99,2},{100,3},{101,4},{102,5},{103,6},{104,7},{105,... | collective-permute-start | bytes 983048 | tf_op jit(solution)/shard_map/ppermute | solution.py:16
  64.4 14.8 %collective-permute-start.2 = (bf16[256,640]{1,0:T(8,128)(2,1)S(1)}, bf16[256,640]{1,0:T(8,128)(2,1)}, u32[]{:S(2)}, u32[]{:S(2)}) collective-permute-start(bf16[256,640]{1,0:T(8,128)(2,1)S(1)} %copy-done.12), channel_id=1, source_target_pairs={{65,0},{66,1},{67,2},{68,3},{69,4},{70,5},{71,6},{72,7},{73,8},{74... | collective-permute-start | bytes 983048 | tf_op jit(solution)/shard_map/ppermute | solution.py:16
  81.6 2.6 %copy-start.9 = (bf16[512,640]{0,1:T(8,128)(2,1)S(1)}, bf16[512,640]{0,1:T(8,128)(2,1)}, u32[]{:S(2)}) copy-start(bf16[512,640]{0,1:T(8,128)(2,1)} %copy.24) | copy-start | bytes 1966084
  84.2 10.9 %copy-start.14 = (f32[10,512]{1,0:T(8,128)S(1)}, f32[10,512]{1,0:T(8,128)}, u32[]{:S(2)}) copy-start(f32[10,512]{1,0:T(8,128)} %get-tuple-element.27) | copy-start | bytes 61444
  84.2 11.0 %copy-start.6 = (f32[10,64,512]{2,1,0:T(8,128)S(1)}, f32[10,64,512]{2,1,0:T(8,128)}, u32[]{:S(2)}) copy-start(f32[10,64,512]{2,1,0:T(8,128)} %fusion.7) | copy-start | bytes 3932164
  84.2 11.0 %copy-start.7 = (bf16[1024,640]{0,1:T(8,128)(2,1)S(1)}, bf16[1024,640]{0,1:T(8,128)(2,1)}, u32[]{:S(2)}) copy-start(bf16[1024,640]{0,1:T(8,128)(2,1)} %copy.29) | copy-start | bytes 3932164
  95.1 9.0 %copy-start.18 = (bf16[640,1280]{1,0:T(8,128)(2,1)S(1)}, bf16[640,1280]{1,0:T(8,128)(2,1)}, u32[]{:S(2)}) copy-start(bf16[640,1280]{1,0:T(8,128)(2,1)} %param.17) | copy-start | bytes 4915204
  106.8 1.1 copy-start.5
  107.9 5.7 %copy-start.16 = (s32[256]{0:T(256)S(1)}, s32[256]{0:T(256)}, u32[]{:S(2)}) copy-start(s32[256]{0:T(256)} %param.25) | copy-start | bytes 3076
  108.7 9.2 %collective-permute-start.10 = (bf16[256,640]{1,0:T(8,128)(2,1)}, bf16[256,640]{1,0:T(8,128)(2,1)}, u32[]{:S(2)}, u32[]{:S(2)}) collective-permute-start(bf16[256,640]{1,0:T(8,128)(2,1)} %get-tuple-element.12), channel_id=1, source_target_pairs={{96,0},{97,1},{98,2},{99,3},{100,4},{101,5},{102,6},{103,7},{104,8... | collective-permute-start | bytes 983048 | tf_op jit(solution)/shard_map/ppermute | solution.py:16
  109.8 11.8 %collective-permute-start.8 = (bf16[256,640]{1,0:T(8,128)(2,1)}, bf16[256,640]{1,0:T(8,128)(2,1)}, u32[]{:S(2)}, u32[]{:S(2)}) collective-permute-start(bf16[256,640]{1,0:T(8,128)(2,1)} %get-tuple-element.14), channel_id=1, source_target_pairs={{96,0},{97,1},{98,2},{99,3},{100,4},{101,5},{102,6},{103,7},{104,8... | collective-permute-start | bytes 983048 | tf_op jit(solution)/shard_map/ppermute | solution.py:16
  112.8 9.8 %collective-permute-start.11 = (bf16[256,640]{1,0:T(8,128)(2,1)S(1)}, bf16[256,640]{1,0:T(8,128)(2,1)}, u32[]{:S(2)}, u32[]{:S(2)}) collective-permute-start(bf16[256,640]{1,0:T(8,128)(2,1)S(1)} %get-tuple-element.11), channel_id=1, source_target_pairs={{32,0},{33,1},{34,2},{35,3},{36,4},{37,5},{38,6},{39,7},{40,8},{41... | collective-permute-start | bytes 983048 | tf_op jit(solution)/shard_map/ppermute | solution.py:16
  112.8 14.8 %collective-permute-start.9 = (bf16[256,640]{1,0:T(8,128)(2,1)S(1)}, bf16[256,640]{1,0:T(8,128)(2,1)}, u32[]{:S(2)}, u32[]{:S(2)}) collective-permute-start(bf16[256,640]{1,0:T(8,128)(2,1)S(1)} %get-tuple-element.13), channel_id=1, source_target_pairs={{32,0},{33,1},{34,2},{35,3},{36,4},{37,5},{38,6},{39,7},{40,8},{41... | collective-permute-start | bytes 983048 | tf_op jit(solution)/shard_map/ppermute | solution.py:16
  123.7 61.5 %copy-start.11 = (bf16[2,256,640]{2,1,0:T(8,128)(2,1)}, bf16[2,256,640]{2,1,0:T(8,128)(2,1)S(1)}, u32[]{:S(2)}) copy-start(bf16[2,256,640]{2,1,0:T(8,128)(2,1)S(1)} %bitcast_dynamic-update-slice_fusion) | copy-start | bytes 1966084
  128.6 56.6 %copy-start.10 = (bf16[2,256,640]{2,1,0:T(8,128)(2,1)}, bf16[2,256,640]{2,1,0:T(8,128)(2,1)S(1)}, u32[]{:S(2)}) copy-start(bf16[2,256,640]{2,1,0:T(8,128)(2,1)S(1)} %bitcast_dynamic-update-slice_fusion.2) | copy-start | bytes 1966084
  180.6 6.7 %copy-start.13 = (f32[1280]{0:T(1024)S(1)}, f32[1280]{0:T(1024)}, u32[]{:S(2)}) copy-start(f32[1280]{0:T(1024)} %param.19) | copy-start | bytes 15364
  185.2 2.5 %copy-start.2 = (f32[512,1280]{1,0:T(8,128)S(1)}, f32[512,1280]{1,0:T(8,128)}, u32[]{:S(2)}) copy-start(f32[512,1280]{1,0:T(8,128)} %reduce_sum.77) | copy-start | bytes 7864324
  188.6 1.8 copy-start.1
Sparse Core Ops, SparseCore 0:
  107.0 73.5 all-gather.2
